TPU v7x, 32 devices: a whole 2x2x4 slice. The times are simulated.
32 devices in a mesh: prow: 8 (over y, x, core), pcol: 4 (over z).
Axes of the slice: x: 2, y: 2, z: 4, core: 2. Of those that a mesh axis runs over, the one named last changes fastest.
Arguments:
- matrix: float32 [8192, 8192], P('prow', 'pcol'), as said below
- pivots: int32 [2, 128], replicated, may hold values from 0 to 8191, as said below
Outputs:
- factored: float32 [8192, 8192], P('prow', 'pcol')
Inputs may be any that keep to these rules, and one draw needn't show every extreme that they name: pivots[s, j] lies between s * 128 + j and 8191; with these interchanges no further pivoting is needed for the 2 panels. `matrix`: all entries are finite. After the given interchanges, the leading 2 * 128 rows and columns of A factor without further interchanges.
All inputs are finite; a program needn't handle non-finite values.
Results may differ from a plain program's by a relative error of at most 0.0003.
Values sent between devices are 32-bit elements; how exact they have to be, the bound alone decides.
No kernel may reach another device: no remote copies, remote signals or barrier semaphores. Data moves between devices by JAX's collectives and lax.ppermute only.
A program may use at most 128 MiB of HBM per device.

v0:
```python
import jax
import jax.numpy as jnp
from jax import lax
from jax.sharding import PartitionSpec as P

NB = 128


def spread(value, axis, source):
    kept = jnp.where(lax.axis_index(axis) == source, value, 0).astype(value.dtype)
    return lax.psum(kept, axis)


def matmul(left_side, right_side):
    return jnp.dot(
        left_side, right_side, precision=lax.Precision.HIGHEST, preferred_element_type=jnp.float32
    )


def small_factor(square):
    size = square.shape[0]
    positions = jnp.arange(size, dtype=jnp.int32)
    identity = (positions[:, None] == positions[None, :]).astype(square.dtype)
    work = square
    for k in range(size):
        under = positions > k
        column = jnp.where(under, work[:, k] / work[k, k], 0.0)
        pivot_row = jnp.where(under, work[k, :], 0.0)
        work = work - column[:, None] * pivot_row[None, :]
        work = work.at[:, k].set(jnp.where(under, column, work[:, k]))
    lower_inv = identity
    for k in range(size):
        multiplier = jnp.where(positions > k, work[:, k], 0.0)
        lower_inv = lower_inv - multiplier[:, None] * lower_inv[k][None, :]
    upper_inv = identity
    for k in range(size - 1, -1, -1):
        scaled_row = upper_inv[k] / work[k, k]
        upper_inv = upper_inv.at[k].set(scaled_row)
        multiplier = jnp.where(positions < k, work[:, k], 0.0)
        upper_inv = upper_inv - multiplier[:, None] * scaled_row[None, :]
    return (work, lower_inv, upper_inv)


def factor_recursive(square):
    size = square.shape[0]
    if size <= 8:
        return small_factor(square)
    half = size // 2
    first_factors, first_lower_inv, first_upper_inv = factor_recursive(square[:half, :half])
    lower_left = matmul(square[half:, :half], first_upper_inv)
    upper_right = matmul(first_lower_inv, square[:half, half:])
    schur = square[half:, half:] - matmul(lower_left, upper_right)
    second_factors, second_lower_inv, second_upper_inv = factor_recursive(schur)
    zeros_upper = jnp.zeros((half, size - half), square.dtype)
    zeros_lower = jnp.zeros((size - half, half), square.dtype)
    factors = jnp.concatenate(
        [
            jnp.concatenate([first_factors, upper_right], axis=1),
            jnp.concatenate([lower_left, second_factors], axis=1),
        ],
        axis=0,
    )
    lower_mixed = -matmul(second_lower_inv, matmul(lower_left, first_lower_inv))
    lower_inv = jnp.concatenate(
        [
            jnp.concatenate([first_lower_inv, zeros_upper], axis=1),
            jnp.concatenate([lower_mixed, second_lower_inv], axis=1),
        ],
        axis=0,
    )
    upper_mixed = -matmul(first_upper_inv, matmul(upper_right, second_upper_inv))
    upper_inv = jnp.concatenate(
        [
            jnp.concatenate([first_upper_inv, upper_mixed], axis=1),
            jnp.concatenate([zeros_lower, second_upper_inv], axis=1),
        ],
        axis=0,
    )
    return (factors, lower_inv, upper_inv)


def swap_plan(pivot_list, top_start):
    width = pivot_list.shape[0]
    order_ids = jnp.arange(width, dtype=jnp.int32)
    earlier = order_ids[:, None] < order_ids[None, :]
    later_rows = order_ids[:, None] > order_ids[None, :]
    same_pivot = pivot_list[:, None] == pivot_list[None, :]
    prior = jnp.max(jnp.where(same_pivot & earlier, order_ids[:, None], -1), axis=0)
    hits_top = (pivot_list[:, None] == top_start + order_ids[None, :]) & earlier
    parent = jnp.max(jnp.where(hits_top, order_ids[:, None], -1), axis=0)
    parent = jnp.where(parent >= 0, parent, order_ids)
    for jump_count in range(width.bit_length()):
        parent = jnp.take(parent, parent)
    source = jnp.where(prior >= 0, top_start + jnp.take(parent, jnp.maximum(prior, 0)), pivot_list)
    final_use = jnp.logical_not(jnp.any(same_pivot & later_rows, axis=0))
    leaving = final_use & (pivot_list >= top_start + width)
    return (source, parent, leaving)


def local(matrix, pivots):
    rows_dev, cols_dev = matrix.shape
    steps_total = pivots.shape[0]
    grid_rows = lax.axis_size("prow")
    grid_cols = lax.axis_size("pcol")
    row_rank = lax.axis_index("prow")
    col_rank = lax.axis_index("pcol")
    local_row = jnp.arange(rows_dev, dtype=jnp.int32)
    local_col = jnp.arange(cols_dev, dtype=jnp.int32)
    global_row = (local_row // NB * grid_rows + row_rank) * NB + local_row % NB
    global_col = (local_col // NB * grid_cols + col_rank) * NB + local_col % NB

    def owned_local(positions):
        mine = positions // NB % grid_rows == row_rank
        return (mine, positions // NB // grid_rows * NB + positions % NB)

    def make_plan(step):
        pivot_list = pivots[step]
        source, root, leaving = swap_plan(pivot_list, step * NB)
        source_mine, source_place = owned_local(source)
        source_local = jnp.where(source_mine, source_place, 0)
        dest_mine, dest_place = owned_local(pivot_list)
        dest_local = jnp.where(leaving & dest_mine, dest_place, rows_dev)
        return (source_mine, source_local, root, dest_local)

    def swap_slabs(slabs, plan, step):
        source_mine, source_local, root, dest_local = plan
        top_owner = step % grid_rows
        top_local = step // grid_rows * NB
        is_top = row_rank == top_owner
        picked = jnp.concatenate([jnp.take(slab, source_local, axis=0) for slab in slabs], axis=1)
        picked = jnp.where(source_mine[:, None], picked, 0.0)
        old_block = jnp.concatenate([slab[top_local : top_local + NB] for slab in slabs], axis=1)
        old_block = jnp.take(old_block, root, axis=0)
        new_top = lax.psum(picked, "prow")
        old_top = spread(old_block, "prow", top_owner)
        moved = []
        offset = 0
        for slab in slabs:
            width = slab.shape[1]
            placed = slab.at[dest_local].set(old_top, mode="drop")
            present_top = placed[top_local : top_local + NB]
            placed = placed.at[top_local : top_local + NB].set(
                jnp.where(is_top, new_top, present_top)
            )
            moved.append(placed)
            offset = offset + width
        return (moved, new_top)

    def factor_panel(lead_slab, top_lead, step):
        panel_owner = step % grid_cols
        factors, own_lower_inv, upper_inv = factor_recursive(top_lead)
        own_lower = matmul(lead_slab, upper_inv)
        lower_part, lower_inv = (
            spread(own_lower, "pcol", panel_owner),
            spread(own_lower_inv, "pcol", panel_owner),
        )
        return (lower_part, lower_inv, factors)

    def split(whole, step):
        low = step // grid_cols * NB
        high = low + NB
        rest = []
        rest.append((high, whole[:, high:]))
        return (whole[:, low:high], rest)

    def join(lead, rest, step):
        low = step // grid_cols * NB
        before = [pair[1] for pair in rest if pair[0] < low]
        after = [pair[1] for pair in rest if pair[0] > low]
        return jnp.concatenate(before + [lead] + after, axis=1)

    def advance(lead, rest, step):
        plan = make_plan(step)
        lead_list, top_lead = swap_slabs([lead], plan, step)
        panel = factor_panel(lead_list[0], top_lead, step)
        rest_list, top_rest = swap_slabs([pair[1] for pair in rest], plan, step)
        low = step // grid_cols * NB
        new_top = jnp.concatenate([top_rest[:, :low], top_lead, top_rest], axis=1)
        rest = [(pair[0], slab) for pair, slab in zip(rest, rest_list)]
        return (lead_list[0], rest, new_top, panel)

    lead, rest = split(matrix, 0)
    lead, rest, new_top, panel = advance(lead, rest, 0)
    current = matrix
    for step in range(steps_total):
        current = join(lead, rest, step)
        lower_part, lower_inv, factors = panel
        upper_rows = matmul(lower_inv, new_top)
        start_row = (step + 1) * NB
        lower_used = jnp.where((global_row >= start_row)[:, None], lower_part, 0.0)
        later = step + 1 < steps_total
        finish_new_top = new_top
        finish_start_row = (step + 1) * NB
        finish_top_owner = step % grid_rows
        finish_top_local = step // grid_rows * NB
        col_live = (global_col >= finish_start_row)[None, :]
        updated = current - matmul(lower_used, jnp.where(col_live, upper_rows, 0.0))
        top_value = jnp.where(col_live, upper_rows, finish_new_top)
        panel_low = step // grid_cols * NB
        finish_offset = panel_low - 0
        owner = col_rank == step % grid_cols
        row_live = (global_row >= finish_start_row)[:, None]
        band = updated[:, finish_offset : finish_offset + NB]
        updated = updated.at[:, finish_offset : finish_offset + NB].set(
            jnp.where(owner & row_live, lower_part, band)
        )
        top_band = top_value[:, finish_offset : finish_offset + NB]
        top_value = top_value.at[:, finish_offset : finish_offset + NB].set(
            jnp.where(owner, factors, top_band)
        )
        finish_present_top = updated[finish_top_local : finish_top_local + NB]
        current = updated.at[finish_top_local : finish_top_local + NB].set(
            jnp.where(row_rank == finish_top_owner, top_value, finish_present_top)
        )
        if later:
            next_lead, next_rest = split(current, step + 1)
        if later:
            lead, rest, new_top, panel = advance(next_lead, next_rest, step + 1)
    return current


def solution(mesh):
    return jax.shard_map(
        local,
        mesh=mesh,
        in_specs=(P("prow", "pcol"), P()),
        out_specs=P("prow", "pcol"),
        check_vma=False,
    )
```

profile of v0, /device:TPU:23, one launch (start us, length us, event | category | flops | bytes accessed | tf_op | source)
XLA Modules:
  0.0 1514.5 jit_solution(13170412135502118320)
XLA Ops:
  7.8 7.0 slice.14693
  43.3 4.6 gather_fusion.12
  55.6 56.0 %all-reduce.71.cloned.1.call-done = (f32[128,1920]{1,0:T(8,128)}, f32[128,1920]{1,0:T(8,128)}, f32[128,128]{1,0:T(8,128)}, f32[128,128]{1,0:T(8,128)}) async-done(((f32[128,1920]{1,0:T(8,128)}, f32[128,1920]{1,0:T(8,128)}, f32[128,128]{1,0:T(8,128)}, f32[128,128]{1,0:T(8,128)}), (f32[128,1920]{1,0:T(8,128)}, f32[128,1920]{1,0:T(8,128)}, f32[128,128]{1,0:T(8,128)}, ...) | async-done | bytes 2097168 | tf_op jit(solution)/shard_map/psum | solution.py:11
  113.6 1.4 fusion.568
  115.7 1.9 select_select_fusion.235
  128.1 1.4 select_select_fusion.231
  165.7 1.4 select_select_fusion.224
  204.5 1.4 select_select_fusion.217
  240.6 1.4 select_select_fusion.210
  466.8 1.4 select_select_fusion.168
  577.8 1.4 select_select_fusion.147
  714.6 1.4 convolution_select_fusion.1
  716.8 7.6 scatter_fusion.1
  724.4 2.6 constant_dynamic-update-slice_fusion
  727.0 27.6 %all-reduce.75.cloned.1.call-done = (f32[128,128]{1,0:T(8,128)}, f32[1024,128]{1,0:T(8,128)}) async-done(((f32[128,128]{1,0:T(8,128)}, f32[1024,128]{1,0:T(8,128)}), (f32[128,128]{1,0:T(8,128)}, f32[1024,128]{1,0:T(8,128)})) %all-reduce.75.cloned.1.call-update) | async-done | bytes 589840 | tf_op jit(solution)/shard_map/psum | solution.py:11
  754.6 1.8 broadcast_select_fusion.1
  757.3 9.8 maximum_subtract_fusion
  768.5 3.9 slice.16906
  775.9 4.6 gather_fusion.25
  783.3 61.8 %all-reduce.69.cloned.1.call-done = (f32[128,1920]{1,0:T(8,128)}, f32[128,1920]{1,0:T(8,128)}, f32[128,128]{1,0:T(8,128)}, f32[128,128]{1,0:T(8,128)}) async-done(((f32[128,1920]{1,0:T(8,128)}, f32[128,1920]{1,0:T(8,128)}, f32[128,128]{1,0:T(8,128)}, f32[128,128]{1,0:T(8,128)}), (f32[128,1920]{1,0:T(8,128)}, f32[128,1920]{1,0:T(8,128)}, f32[128,128]{1,0:T(8,128)}, ...) | async-done | bytes 2097168 | tf_op jit(solution)/shard_map/psum | solution.py:11
  847.1 1.4 fusion.576
  849.3 1.9 select_select_fusion.123
  1123.9 1.4 select_select_fusion.70
  1348.0 1.4 select_select_fusion.28
  1448.2 1.4 convolution_select_fusion
  1449.7 7.6 scatter_fusion.3
  1457.3 2.6 constant_dynamic-update-slice_fusion.2
  1459.9 28.3 %all-reduce.73.cloned.1.call-done = (f32[128,128]{1,0:T(8,128)}, f32[1024,128]{1,0:T(8,128)}) async-done(((f32[128,128]{1,0:T(8,128)}, f32[1024,128]{1,0:T(8,128)}), (f32[128,128]{1,0:T(8,128)}, f32[1024,128]{1,0:T(8,128)})) %all-reduce.73.cloned.1.call-update) | async-done | bytes 589840 | tf_op jit(solution)/shard_map/psum | solution.py:11
  1488.2 1.8 broadcast_select_fusion
  1490.9 9.9 maximum_subtract_fusion.1
  1501.7 3.4 copy-done
  1505.1 2.4 fusion
  (3529 shorter events, 1228.3 us)
Async XLA Ops:
  6.5 105.0 %all-reduce.71.cloned.1.call-start = ((), (), s32[]{:S(2)}) async-start(), calls=%async_computation.1 | async-start | bytes 4194304 | tf_op jit(solution)/shard_map/psum | solution.py:11
  7.8 8.9 copy-start.9
  50.4 704.2 %all-reduce.75.cloned.1.call-start = ((), (), s32[]{:S(2)}) async-start(), calls=%async_computation.3 | async-start | bytes 1179648 | tf_op jit(solution)/shard_map/psum | solution.py:11
  111.6 596.8 %copy-start.7 = (f32[128,128]{1,0:T(8,128)S(1)}, f32[128,128]{1,0:T(8,128)}, u32[]{:S(2)}) copy-start(f32[128,128]{1,0:T(8,128)} %get-tuple-element.6764) | copy-start | bytes 196612
  111.6 598.0 %copy-start.3 = (f32[128,128]{1,0:T(8,128)S(1)}, f32[128,128]{1,0:T(8,128)}, u32[]{:S(2)}) copy-start(f32[128,128]{1,0:T(8,128)} %get-tuple-element.6765) | copy-start | bytes 196612
  162.7 554.1 %copy-start.5 = (f32[128,1920]{1,0:T(8,128)S(1)}, f32[128,1920]{1,0:T(8,128)}, u32[]{:S(2)}) copy-start(f32[128,1920]{1,0:T(8,128)} %get-tuple-element.6762) | copy-start | bytes 2949124
  716.1 129.0 %all-reduce.69.cloned.1.call-start = ((), (), s32[]{:S(2)}) async-start(), calls=%async_computation | async-start | bytes 4194304 | tf_op jit(solution)/shard_map/psum | solution.py:11
  757.3 9.9 copy-start.1
  783.1 705.1 %all-reduce.73.cloned.1.call-start = ((), (), s32[]{:S(2)}) async-start(), calls=%async_computation.2 | async-start | bytes 1179648 | tf_op jit(solution)/shard_map/psum | solution.py:11
  845.1 597.1 %copy-start.8 = (f32[128,128]{1,0:T(8,128)S(1)}, f32[128,128]{1,0:T(8,128)}, u32[]{:S(2)}) copy-start(f32[128,128]{1,0:T(8,128)} %get-tuple-element.6760) | copy-start | bytes 196612
  845.1 598.2 %copy-start.4 = (f32[128,128]{1,0:T(8,128)S(1)}, f32[128,128]{1,0:T(8,128)}, u32[]{:S(2)}) copy-start(f32[128,128]{1,0:T(8,128)} %get-tuple-element.6761) | copy-start | bytes 196612
  896.8 552.9 %copy-start.6 = (f32[128,1920]{1,0:T(8,128)S(1)}, f32[128,1920]{1,0:T(8,128)}, u32[]{:S(2)}) copy-start(f32[128,1920]{1,0:T(8,128)} %get-tuple-element.6758) | copy-start | bytes 2949124
  1490.9 9.9 copy-start.2
  1501.7 3.4 copy-start
Sparse Core Ops, SparseCore 0:
  50.5 60.9 all-reduce.70
  716.2 38.3 all-reduce.74
  783.2 61.8 all-reduce.68
  1449.8 38.3 all-reduce.72
where the time goes:
time: 1540 us; the launch traced here: 1510 us
  other arithmetic  931 us (60%)
  local copies, waits for them, and re-layouts  312 us (20%)
  waiting for transfers between devices  174 us (11%)
  matrix products  75.5 us (5%)
  between operations  21.9 us (1%)
    another operation x232, other arithmetic  301 us
    select_n x256, other arithmetic, small_factor(): column = jnp.where(under, work[:, k] / work[k, k], 0.0)  204 us
    psum x4, waiting for transfers between devices, spread(): return lax.psum(kept, axis)  174 us
    slice x256, local copies, waits for them, and re-layouts, small_factor(): column = jnp.where(under, work[:, k] / work[k, k], 0.0)  166 us
    mul x255, other arithmetic, small_factor(): upper_inv = upper_inv - multiplier[:, None] * scaled_row[None, :]  162 us
    div x224, other arithmetic, small_factor(): scaled_row = upper_inv[k] / work[k, k]  142 us
    dot_general x216, matrix products, matmul(): jnp.dot(left_side, right_side, precision=lax.Precision.HIGHEST, preferred...  75.5 us
    slice x64, local copies, waits for them, and re-layouts, small_factor(): scaled_row = upper_inv[k] / work[k, k]  39.4 us
  transfers between devices with their start and end apart: 4, of which 4 were waited for; matrix products, arithmetic and copies ran while one was open for 2% of the time, Pallas kernels for 0%

commit v1 on v0

v1 whole, which is shorter than its diff:
```python
import functools

import jax
import jax.numpy as jnp
from jax import lax
from jax.experimental import pallas as pl
from jax.experimental.pallas import tpu as pltpu
from jax.sharding import PartitionSpec as P

NB = 128
TILE = 8
VMEM = pltpu.VMEM
SMEM = pltpu.SMEM
ANY = pl.ANY


def dot_full(left, right):
    return jnp.dot(left, right, precision=lax.Precision.HIGHEST, preferred_element_type=jnp.float32)


def split_bf16(value):
    high = value.astype(jnp.bfloat16)
    low = (value - high.astype(jnp.float32)).astype(jnp.bfloat16)
    return high, low


def dot_bf16(left, right):
    return jnp.dot(left, right, preferred_element_type=jnp.float32)


def pick_kernel(grid_rows, piv_ref, rank_ref, mat_ref, pick_ref, place_ref, root_ref, table_ref, sem):
    lead = piv_ref.shape[0]
    me = rank_ref[0]

    def prepare(j, carry):
        table_ref[piv_ref[j]] = piv_ref[j]
        return carry

    lax.fori_loop(0, lead, prepare, 0, unroll=8)

    def prepare_top(j, carry):
        table_ref[j] = j
        return carry

    lax.fori_loop(0, lead, prepare_top, 0, unroll=8)
    pick_ref[...] = jnp.zeros_like(pick_ref)

    def owned(row):
        block = row >> (NB.bit_length() - 1)
        if grid_rows & (grid_rows - 1) == 0:
            turn, rank = block >> (grid_rows.bit_length() - 1), block & (grid_rows - 1)
        else:
            turn, rank = lax.div(block, grid_rows), lax.rem(block, grid_rows)
        return rank == me, turn * NB + (row & (NB - 1))

    def copy_of(place, j):
        return pltpu.make_async_copy(mat_ref.at[pl.ds(place, 1)], pick_ref.at[pl.ds(j, 1)], sem)

    def exchange(j, count):
        other = piv_ref[j]
        upper = table_ref[j]
        lower = table_ref[other]
        table_ref[other] = upper
        table_ref[j] = lower
        mine, place = owned(lower)

        @pl.when(mine)
        def _():
            copy_of(place, j).start()

        return count + mine.astype(jnp.int32)

    count = lax.fori_loop(0, lead, exchange, 0)

    def leave(j, carry):
        other = piv_ref[j]
        mine, place = owned(other)
        place_ref[j] = jnp.where(mine & (other >= lead), place, -1)
        root_ref[j] = jnp.where(other >= lead, table_ref[other], 0)
        return carry

    lax.fori_loop(0, lead, leave, 0)

    def finish(j, carry):
        copy_of(0, 0).wait()
        return carry

    lax.fori_loop(0, count, finish, 0)


def pick_rows(matrix, pivots, row_rank, grid_rows):
    rows_dev, cols_dev = matrix.shape
    lead = pivots.shape[0] * pivots.shape[1]
    return pl.pallas_call(
        functools.partial(pick_kernel, grid_rows),
        out_shape=(
            jax.ShapeDtypeStruct((lead, cols_dev), jnp.float32),
            jax.ShapeDtypeStruct((lead,), jnp.int32),
            jax.ShapeDtypeStruct((lead,), jnp.int32),
        ),
        in_specs=[
            pl.BlockSpec(memory_space=SMEM),
            pl.BlockSpec(memory_space=SMEM),
            pl.BlockSpec(memory_space=ANY),
        ],
        out_specs=(
            pl.BlockSpec(memory_space=VMEM),
            pl.BlockSpec(memory_space=SMEM),
            pl.BlockSpec(memory_space=SMEM),
        ),
        scratch_shapes=[SMEM((rows_dev * grid_rows,), jnp.int32), pltpu.SemaphoreType.DMA],
        name="pick_rows",
    )(pivots.reshape(-1), row_rank.reshape(1), matrix)


def lu_tiles(square):
    size = square.shape[0]
    groups = size // TILE
    sub = lax.broadcasted_iota(jnp.int32, (TILE, size), 0)
    lane = lax.broadcasted_iota(jnp.int32, (TILE, size), 1)
    work = [square[g * TILE : (g + 1) * TILE] for g in range(groups)]
    left = [(lane == sub + g * TILE).astype(jnp.float32) for g in range(groups)]
    right = list(left)
    scale = jnp.zeros((TILE, size), jnp.float32)
    for k in range(size):
        own, i = k // TILE, k % TILE
        row = jnp.broadcast_to(work[own][i : i + 1], (TILE, size))
        row_left = jnp.broadcast_to(left[own][i : i + 1], (TILE, size))
        pivot = jnp.broadcast_to(row[:, k : k + 1], (TILE, size))
        inverse = 1.0 / pivot
        scale = jnp.where(lane == k, inverse, scale)
        row = jnp.where(lane > k, row, 0.0)
        row_scaled = row * inverse
        for g in range(own + 1):
            column = jnp.broadcast_to(right[g][:, k : k + 1], (TILE, size))
            right[g] = right[g] - column * row_scaled
        for g in range(own, groups):
            if g == own and i == TILE - 1:
                continue
            column = jnp.broadcast_to(work[g][:, k : k + 1], (TILE, size)) * inverse
            updated = work[g] - column * row
            if g == own:
                under = sub > i
                column = jnp.where(under, column, 0.0)
                updated = jnp.where(under, updated, work[g])
                work[g] = jnp.where((lane == k) & under, column, updated)
            else:
                work[g] = jnp.where(lane == k, column, updated)
            left[g] = left[g] - column * row_left
    right = [tile * scale for tile in right]
    return jnp.concatenate(work, 0), jnp.concatenate(left, 0), jnp.concatenate(right, 0)


def factor_kernel(block_ref, fac_ref, low_ref, up_ref):
    size = block_ref.shape[0]
    half = NB
    fac0, low0, up0 = lu_tiles(block_ref[:half, :half])
    upper = dot_full(low0, block_ref[:half, half:])
    lower = dot_full(block_ref[half:, :half], up0)
    schur = block_ref[half:, half:] - dot_full(lower, upper)
    fac1, low1, up1 = lu_tiles(schur)
    zeros = jnp.zeros((half, size - half), jnp.float32)
    fac_ref[:half, :half] = fac0
    fac_ref[:half, half:] = upper
    fac_ref[half:, :half] = lower
    fac_ref[half:, half:] = fac1
    low_ref[:half, :half] = low0
    low_ref[:half, half:] = zeros
    low_ref[half:, :half] = -dot_full(low1, dot_full(lower, low0))
    low_ref[half:, half:] = low1
    up_ref[:half, :half] = up0
    up_ref[:half, half:] = -dot_full(dot_full(up0, upper), up1)
    up_ref[half:, :half] = zeros
    up_ref[half:, half:] = up1


def factor(block):
    shape = jax.ShapeDtypeStruct(block.shape, jnp.float32)
    return pl.pallas_call(
        factor_kernel,
        out_shape=(shape, shape, shape),
        in_specs=[pl.BlockSpec(memory_space=VMEM)],
        out_specs=tuple(pl.BlockSpec(memory_space=VMEM) for _ in range(3)),
        name="factor",
    )(block)


def update_kernel(
    rank_ref, place_ref, root_ref, mat_ref, panel_ref, top_ref, old_ref, old_panel_ref, fac_ref, low_ref, up_ref,
    out_ref, work_ref, uf_ref, uh_ref, ul_ref, lp_ref, in_sem, out_sem,
):
    rows, cols = work_ref.shape
    lead = top_ref.shape[0]
    steps = lead // NB
    chunks = rows // NB
    row_rank, col_rank = rank_ref[0], rank_ref[1]

    def chunk(c):
        return pl.ds(c * NB, NB)

    def load(c):
        return pltpu.make_async_copy(mat_ref.at[chunk(c)], work_ref.at[chunk(c)], in_sem.at[c])

    def save(c):
        return pltpu.make_async_copy(work_ref.at[chunk(c)], out_ref.at[chunk(c)], out_sem.at[c])

    for c in range(chunks):
        load(c).start()
    upper = dot_full(low_ref[...], top_ref[...])
    uf_ref[...] = upper
    high, low = split_bf16(upper)
    uh_ref[...] = high
    ul_ref[...] = low
    lp_ref[...] = panel_ref[...]
    for c in range(chunks):
        load(c).wait()

    def place_row(j, carry):
        place = place_ref[j]

        @pl.when(place >= 0)
        def _():
            root = root_ref[j]
            lp_ref[pl.ds(place, 1), :] = old_panel_ref[pl.ds(root, 1), :]
            work_ref[pl.ds(place, 1), :] = old_ref[pl.ds(root, 1), :]

        return carry

    lax.fori_loop(0, lead, place_row, 0)
    for c in range(chunks):
        part = dot_full(lp_ref[c * NB : (c + 1) * NB], up_ref[...])
        lp_ref[c * NB : (c + 1) * NB] = part
        high, low = split_bf16(part)
        delta = dot_bf16(high, uh_ref[...]) + (dot_bf16(high, ul_ref[...]) + dot_bf16(low, uh_ref[...]))
        work_ref[c * NB : (c + 1) * NB] = work_ref[c * NB : (c + 1) * NB] - delta
        for s in range(steps):

            @pl.when(col_rank == s)
            def _():
                work_ref[c * NB : (c + 1) * NB, :NB] = lp_ref[c * NB : (c + 1) * NB, s * NB : (s + 1) * NB]

        if c == 0:
            for s in range(steps):

                @pl.when(row_rank == s)
                def _():
                    work_ref[:NB] = uf_ref[s * NB : (s + 1) * NB]
                    for q in range(steps):

                        @pl.when(col_rank == q)
                        def _():
                            work_ref[:NB, :NB] = fac_ref[s * NB : (s + 1) * NB, q * NB : (q + 1) * NB]

        save(c).start()
    for c in range(chunks):
        save(c).wait()


def update(ranks, place, root, matrix, panel, top, old, old_panel, fac, low, up):
    rows, cols = matrix.shape
    lead = top.shape[0]
    chunks = rows // NB
    in_vmem = pl.BlockSpec(memory_space=VMEM)
    in_smem = pl.BlockSpec(memory_space=SMEM)
    anywhere = pl.BlockSpec(memory_space=ANY)
    return pl.pallas_call(
        update_kernel,
        out_shape=jax.ShapeDtypeStruct(matrix.shape, jnp.float32),
        in_specs=[in_smem] * 3 + [anywhere] + [in_vmem] * 7,
        out_specs=anywhere,
        scratch_shapes=[
            VMEM((rows, cols), jnp.float32),
            VMEM((lead, cols), jnp.float32),
            VMEM((lead, cols), jnp.bfloat16),
            VMEM((lead, cols), jnp.bfloat16),
            VMEM((rows, lead), jnp.float32),
            pltpu.SemaphoreType.DMA((chunks,)),
            pltpu.SemaphoreType.DMA((chunks,)),
        ],
        name="update",
    )(ranks, place, root, matrix, panel, top, old, old_panel, fac, low, up)


def swap_bit(value, axis, bit):
    size = lax.axis_size(axis)
    return lax.ppermute(value, axis, [(i, i ^ bit) for i in range(size)])


def reduce_half(value, axis, bit):
    half = value.shape[0] // 2
    upper = (lax.axis_index(axis) // bit) % 2 == 1
    keep = jnp.where(upper, value[half:], value[:half])
    give = jnp.where(upper, value[:half], value[half:])
    return keep + swap_bit(give, axis, bit)


def gather_half(value, axis, bit, dim=0):
    upper = (lax.axis_index(axis) // bit) % 2 == 1
    other = swap_bit(value, axis, bit)
    return jnp.concatenate([jnp.where(upper, other, value), jnp.where(upper, value, other)], axis=dim)


def tree(value, axis, bit, first):
    size = lax.axis_size(axis)
    pairs = [(i, i + bit) for i in range(size) if i % (2 * bit) < first and i % (2 * bit) < bit]
    got = lax.ppermute(value, axis, pairs)
    mine = lax.axis_index(axis) % (2 * bit) < first
    return jnp.where(mine, value, got)


def local(matrix, pivots):
    steps = pivots.shape[0]
    grid_rows = lax.axis_size("prow")
    grid_cols = lax.axis_size("pcol")
    row_rank = lax.axis_index("prow")
    col_rank = lax.axis_index("pcol")
    row_bits = [1 << b for b in range(1, grid_rows.bit_length() - 1)]
    col_bits = [1 << b for b in range(1, grid_cols.bit_length() - 1)]
    ranks = jnp.stack([row_rank, col_rank]).astype(jnp.int32)

    panel = matrix[:, :NB]
    for bit in reversed(col_bits):
        panel = tree(panel, "pcol", bit, steps)
    panel = gather_half(panel, "pcol", 1, 1)

    old = matrix[:NB]
    old_panel = matrix[:NB, :NB]
    for bit in reversed(row_bits):
        old_panel = tree(old_panel, "prow", bit, steps)
        old = tree(old, "prow", bit, steps)

    picked, place, root = pick_rows(matrix, pivots, row_rank.astype(jnp.int32), grid_rows)
    block = reduce_half(picked[:, :NB], "prow", 1)
    for bit in row_bits:
        block = block + swap_bit(block, "prow", bit)
    block = jnp.concatenate([block, old_panel], axis=0)
    for bit in reversed(col_bits):
        block = tree(block, "pcol", bit, steps)
    block = gather_half(block, "pcol", 1, 1)
    block = gather_half(block[None], "prow", 1)
    old_panel = block[:, NB:].reshape(steps * NB, steps * NB)
    block = block[:, :NB].reshape(steps * NB, steps * NB)
    fac, low, up = factor(block)

    top = picked
    for bit in [1] + row_bits:
        top = reduce_half(top, "prow", bit)
    for bit in reversed(row_bits):
        top = gather_half(top, "prow", bit)
    both = gather_half(jnp.stack([top, old])[None], "prow", 1)
    top = both[:, 0].reshape(steps * NB, -1)
    old = both[:, 1].reshape(steps * NB, -1)
    return update(ranks, place, root, matrix, panel, top, old, old_panel, fac, low, up)


def solution(mesh):
    return jax.shard_map(
        local,
        mesh=mesh,
        in_specs=(P("prow", "pcol"), P()),
        out_specs=P("prow", "pcol"),
        check_vma=False,
    )
```

time: 1540 us -> 188 us (0.12); the launches traced: 1510 us -> 187 us
  other arithmetic: 931 us -> 17.7 us
  local copies, waits for them, and re-layouts: 312 us -> 5.07 us
  waiting for transfers between devices: 174 us -> 53.5 us
  matrix products: 75.5 us -> 0 us
  Pallas kernels: 0 us -> 66.7 us
  starting transfers between devices: 0.13 us -> 43.9 us
  between operations: 21.9 us -> 0.41 us
    another operation x232 -> x3, other arithmetic: 301 us -> 0.81 us  [the longest x1 0.59 us: local(): ranks = jnp.stack([row_rank, col_rank]).astype(jnp.int32)]
    select_n x349 -> x15, other arithmetic: 252 us -> 8.62 us  [the longest x5 3.63 us: tree(): return jnp.where(mine, value, got)]
    slice x328 -> x3, local copies, waits for them, and re-layouts: 219 us -> 5.07 us  [the longest x1 2.34 us: local(): old = matrix[:NB]]
    psum x4 -> x0, waiting for transfers between devices: 174 us -> none  [spread(): return lax.psum(kept, axis)]
    mul x511 -> x0, other arithmetic: 165 us -> none  [the longest x255 162 us: small_factor(): upper_inv = upper_inv - multiplier[:, None] * scaled_row[None, :]]
    div x224 -> x0, other arithmetic: 142 us -> none  [small_factor(): scaled_row = upper_inv[k] / work[k, k]]
    dot_general x216 -> x0, matrix products: 75.5 us -> none  [matmul(): jnp.dot(left_side, right_side, precision=lax.Precision.HIGHEST, preferred...]
    pallas_call x0 -> x3, Pallas kernels: none -> 66.7 us  [the longest x1 37.2 us: factor(): pl.pallas_call(factor_kernel, out_shape=(shape, shape, shape), in_specs=[...]
  transfers between devices with their start and end apart: 4 -> 18, of which waited for: 4 -> 7; matrix products, arithmetic and copies ran while one was open for 2% -> 8% of each run, Pallas kernels for 0% -> 20%
where the time goes in v1:
time: 188 us; the launch traced here: 187 us
  Pallas kernels  66.7 us (35%)
  waiting for transfers between devices  53.5 us (28%)
  starting transfers between devices  43.9 us (23%)
  other arithmetic  17.7 us (9%)
  local copies, waits for them, and re-layouts  5.07 us (3%)
    ppermute x12, waiting for transfers between devices, swap_bit(): return lax.ppermute(value, axis, [(i, i ^ bit) for i in range(size)])  39.3 us
    pallas_call x1, Pallas kernels, factor(): pl.pallas_call(factor_kernel, out_shape=(shape, shape, shape), in_specs=[...  37.2 us
    ppermute x12, starting transfers between devices, swap_bit(): return lax.ppermute(value, axis, [(i, i ^ bit) for i in range(size)])  36.3 us
    pallas_call x1, Pallas kernels, update(): pl.pallas_call(update_kernel, out_shape=jax.ShapeDtypeStruct(matrix.shape...  20.3 us
    ppermute x6, waiting for transfers between devices, tree(): got = lax.ppermute(value, axis, pairs)  14.2 us
    pallas_call x1, Pallas kernels, pick_rows(): pl.pallas_call(functools.partial(pick_kernel, grid_rows), out_shape=(jax....  9.2 us
    ppermute x6, starting transfers between devices, tree(): got = lax.ppermute(value, axis, pairs)  7.6 us
    concatenate x4, other arithmetic, gather_half(): jnp.concatenate([jnp.where(upper, other, value), jnp.where(upper, value,...  4.2 us
  transfers between devices with their start and end apart: 18, of which 7 were waited for; matrix products, arithmetic and copies ran while one was open for 8% of the time, Pallas kernels for 20%

profile of v1, /device:TPU:23, one launch (start us, length us, event | category | flops | bytes accessed | tf_op | source)
XLA Modules:
  0.0 187.3 jit_solution(12264895888648764409)
XLA Ops:
  0.0 9.2 %pick_rows.1 = (f32[256,2048]{1,0:T(8,128)}, s32[256]{0:T(256)}, s32[256]{0:T(256)}) custom-call(s32[256]{0:T(256)} %bitcast.27, s32[1]{0:T(128)} %bitcast.rank_ref, f32[1024,2048]{1,0:T(8,128)} %mat_ref.3), custom_call_target="tpu_custom_call" | custom-call | tf_op jit(solution)/shard_map/pick_rows/pallas_call | solution.py:94
  9.2 1.8 slice_select_fusion
  13.2 2.3 %slice.63 = f32[128,2048]{1,0:T(8,128)} slice(f32[1024,2048]{1,0:T(8,128)} %mat_ref.3), slice={[0:128], [0:2048]} | slice | bytes 2097152 | tf_op jit(solution)/shard_map/slice | solution.py:326
  15.5 1.6 collective-permute-start.7
  17.2 1.4 select_add_fusion
  21.3 1.3 collective-permute-start.14
  22.7 2.1 %collective-permute-start.11 = (f32[128,128]{1,0:T(8,128)S(1)}, f32[128,128]{1,0:T(8,128)S(1)}, u32[]{:S(2)}, u32[]{:S(2)}) collective-permute-start(f32[128,128]{1,0:T(8,128)S(1)} %select_add_fusion.3), channel_id=1, source_target_pairs={{0,8},{4,12},{8,0},{12,4},{16,24},{20,28},{24,16},{28,20},{1,9},{5... | collective-permute-start | bytes 196616 | tf_op jit(solution)/shard_map/ppermute | solution.py:286
  24.8 8.3 %collective-permute-done.3 = f32[64,2048]{1,0:T(8,128)} collective-permute-done((f32[64,2048]{1,0:T(8,128)}, f32[64,2048]{1,0:T(8,128)}, u32[]{:S(2)}, u32[]{:S(2)}) %collective-permute-start.3) | collective-permute-done | bytes 524320 | tf_op jit(solution)/shard_map/ppermute | solution.py:286
  33.2 1.1 select_add_fusion.1
  34.3 2.3 %collective-permute-start.4 = (f32[32,2048]{1,0:T(8,128)S(1)}, f32[32,2048]{1,0:T(8,128)S(1)}, u32[]{:S(2)}, u32[]{:S(2)}) collective-permute-start(f32[32,2048]{1,0:T(8,128)S(1)} %slice_select_fusion.2), channel_id=1, source_target_pairs={{0,16},{4,20},{8,24},{12,28},{16,0},{20,4},{24,8},{28,12},{1,17},{... | collective-permute-start | bytes 786440 | tf_op jit(solution)/shard_map/ppermute | solution.py:286
  36.6 1.7 broadcast_select_fusion.2
  38.3 1.3 collective-permute-start.8
  39.6 2.4 %collective-permute-done.4 = f32[32,2048]{1,0:T(8,128)S(1)} collective-permute-done((f32[32,2048]{1,0:T(8,128)S(1)}, f32[32,2048]{1,0:T(8,128)S(1)}, u32[]{:S(2)}, u32[]{:S(2)}) %collective-permute-start.4) | collective-permute-done | bytes 262176 | tf_op jit(solution)/shard_map/ppermute | solution.py:286
  42.0 1.2 collective-permute-start.5
  43.6 5.8 %collective-permute-done.12 = f32[128,128]{1,0:T(8,128)S(1)} collective-permute-done((f32[128,128]{1,0:T(8,128)S(1)}, f32[128,128]{1,0:T(8,128)S(1)}, u32[]{:S(2)}, u32[]{:S(2)}) %collective-permute-start.12) | collective-permute-done | bytes 65568 | tf_op jit(solution)/shard_map/ppermute | solution.py:286
  49.5 8.1 %collective-permute-start.6 = (f32[64,2048]{1,0:T(8,128)S(1)}, f32[64,2048]{1,0:T(8,128)S(1)}, u32[]{:S(2)}, u32[]{:S(2)}) collective-permute-start(f32[64,2048]{1,0:T(8,128)S(1)} %pad_maximum_fusion.2), channel_id=1, source_target_pairs={{0,8},{4,12},{8,0},{12,4},{16,24},{20,28},{24,16},{28,20},{1,9},{5... | collective-permute-start | bytes 1572872 | tf_op jit(solution)/shard_map/ppermute | solution.py:286
  57.6 10.9 %collective-permute-done.8 = f32[128,2048]{1,0:T(8,128)S(1)} collective-permute-done((f32[128,2048]{1,0:T(8,128)S(1)}, f32[128,2048]{1,0:T(8,128)S(1)}, u32[]{:S(2)}, u32[]{:S(2)}) %collective-permute-start.8) | collective-permute-done | bytes 1048608 | tf_op jit(solution)/shard_map/ppermute | solution.py:306
  68.7 11.1 %collective-permute-done.6 = f32[64,2048]{1,0:T(8,128)S(1)} collective-permute-done((f32[64,2048]{1,0:T(8,128)S(1)}, f32[64,2048]{1,0:T(8,128)S(1)}, u32[]{:S(2)}, u32[]{:S(2)}) %collective-permute-start.6) | collective-permute-done | bytes 524320 | tf_op jit(solution)/shard_map/ppermute | solution.py:286
  80.0 1.5 maximum_bitcast_fusion
  81.4 1.9 %collective-permute-start.9 = (f32[1,2,128,2048]{3,2,1,0:T(8,128)}, f32[1,2,128,2048]{3,2,1,0:T(8,128)}, u32[]{:S(2)}, u32[]{:S(2)}) collective-permute-start(f32[1,2,128,2048]{3,2,1,0:T(8,128)} %maximum_bitcast_fusion), channel_id=1, source_target_pairs={{0,4},{4,0},{8,12},{12,8},{16,20},{20,16},{24,28},{28,24},{1,5},{5... | collective-permute-start | bytes 6291464 | tf_op jit(solution)/shard_map/ppermute | solution.py:286
  83.4 1.3 collective-permute-start.15
  84.7 1.9 %slice.56 = f32[1024,128]{1,0:T(8,128)} slice(f32[1024,2048]{1,0:T(8,128)} %mat_ref.3), slice={[0:1024], [0:128]} | slice | bytes 1048576 | tf_op jit(solution)/shard_map/slice | solution.py:321
  86.6 1.5 collective-permute-start
  88.1 3.2 %collective-permute-done.15 = f32[256,128]{1,0:T(8,128)S(1)} collective-permute-done((f32[256,128]{1,0:T(8,128)S(1)}, f32[256,128]{1,0:T(8,128)S(1)}, u32[]{:S(2)}, u32[]{:S(2)}) %collective-permute-start.15) | collective-permute-done | bytes 131104 | tf_op jit(solution)/shard_map/ppermute | solution.py:306
  91.3 15.7 %collective-permute-start.16 = (f32[256,128]{1,0:T(8,128)S(1)}, f32[256,128]{1,0:T(8,128)S(1)}, u32[]{:S(2)}, u32[]{:S(2)}) collective-permute-start(f32[256,128]{1,0:T(8,128)S(1)} %broadcast_select_fusion.12), channel_id=1, source_target_pairs={{0,1},{1,0},{2,3},{3,2},{4,5},{5,4},{6,7},{7,6},{8,9},{9,8},{10,11... | collective-permute-start | bytes 393224 | tf_op jit(solution)/shard_map/ppermute | solution.py:286
  107.0 11.7 %collective-permute-done.16 = f32[256,128]{1,0:T(8,128)S(1)} collective-permute-done((f32[256,128]{1,0:T(8,128)S(1)}, f32[256,128]{1,0:T(8,128)S(1)}, u32[]{:S(2)}, u32[]{:S(2)}) %collective-permute-start.16) | collective-permute-done | bytes 131104 | tf_op jit(solution)/shard_map/ppermute | solution.py:286
  119.3 1.1 broadcast_select_fusion.5
  120.4 2.3 %collective-permute-start.1 = (f32[1024,128]{1,0:T(8,128)S(1)}, f32[1024,128]{1,0:T(8,128)S(1)}, u32[]{:S(2)}, u32[]{:S(2)}) collective-permute-start(f32[1024,128]{1,0:T(8,128)S(1)} %broadcast_select_fusion.5), channel_id=1, source_target_pairs={{0,1},{1,0},{2,3},{3,2},{4,5},{5,4},{6,7},{7,6},{8,9},{9,8},{10,11... | collective-permute-start | bytes 1572872 | tf_op jit(solution)/shard_map/ppermute | solution.py:286
  124.2 37.2 %factor.1 = (f32[256,256]{1,0:T(8,128)}, f32[256,256]{1,0:T(8,128)}, f32[256,256]{1,0:T(8,128)}) custom-call(f32[256,256]{1,0:T(8,128)} %bitcast.26), custom_call_target="tpu_custom_call" | custom-call | tf_op jit(solution)/shard_map/factor/pallas_call | solution.py:179
  162.5 2.0 %broadcast_select_fusion = (f32[1,2,128,2048]{3,2,1,0:T(8,128)S(1)}, f32[1,2,128,2048]{3,2,1,0:T(8,128)S(1)}) fusion(f32[1,2,128,2048]{3,2,1,0:T(8,128)} %collective-permute-done.9, pred[]{:T(512)S(6)} %eq.36, f32[1,128,2048]{2,1,0:T(8,128)S(1)} %select_bitcast_fusion, f32[1,128,2048]{2,1,0:T(8,128)S(1)} %maximum_bitcast_fusion.1), kind=kLoop, calls=%fused_computation.9 | loop fusion | flops 1572864 | bytes 8388609 | tf_op jit(solution)/shard_map/jit(_where)/select_n | solution.py:300
  164.6 2.2 %pad_maximum_fusion = (f32[2,1,128,2048]{3,2,1,0:T(8,128)}, f32[2,1,128,2048]{3,2,1,0:T(8,128)}) fusion(f32[1,2,128,2048]{3,2,1,0:T(8,128)S(1)} %get-tuple-element.19, f32[1,2,128,2048]{3,2,1,0:T(8,128)S(1)} %get-tuple-element.20), kind=kLoop, calls=%fused_computation.3 | loop fusion | flops 1048576 | bytes 8388608 | tf_op jit(solution)/shard_map/concatenate | solution.py:300
  166.8 20.3 %update.1 = f32[1024,2048]{1,0:T(8,128)} custom-call(s32[2]{0:T(128)} %pad_add_fusion.rank_ref, s32[256]{0:T(256)} %get-tuple-element.11.place_ref, s32[256]{0:T(256)} %get-tuple-element.12.root_ref, f32[1024,2048]{1,0:T(8,128)} %mat_ref.3, f32[1024,256]{1,0:T(8,128)} %pad_maximum_fusion.1.panel_ref, f32[256,2048]{1,0:T(8,128)} %bitcast.24, ...), custom_call_target="tpu_custom_call" | custom-call | tf_op jit(solution)/shard_map/update/pallas_call | solution.py:266
  (43 shorter events, 9.1 us)
Async XLA Ops:
  9.2 8.0 %copy-start = (f32[256,2048]{1,0:T(8,128)S(1)}, f32[256,2048]{1,0:T(8,128)}, u32[]{:S(2)}) copy-start(f32[256,2048]{1,0:T(8,128)} %get-tuple-element.13) | copy-start | bytes 6291460
  11.0 6.1 %collective-permute-start.2 = (f32[128,2048]{1,0:T(8,128)S(1)}, f32[128,2048]{1,0:T(8,128)}, u32[]{:S(2)}, u32[]{:S(2)}) collective-permute-start(f32[128,2048]{1,0:T(8,128)S(1)} %slice_select_fusion), channel_id=1, source_target_pairs={{0,4},{4,0},{8,12},{12,8},{16,20},{20,16},{24,28},{28,24},{1,5},{5... | collective-permute-start | bytes 3145736 | tf_op jit(solution)/shard_map/ppermute | solution.py:286
  12.5 8.0 %collective-permute-start.13 = (f32[128,128]{1,0:T(8,128)S(1)}, f32[128,128]{1,0:T(8,128)S(1)}, u32[]{:S(2)}, u32[]{:S(2)}) collective-permute-start(f32[128,128]{1,0:T(8,128)S(1)} %slice.68), channel_id=1, source_target_pairs={{0,16},{4,20},{1,17},{5,21},{2,18},{6,22},{3,19},{7,23}} | collective-permute-start | bytes 196616 | tf_op jit(solution)/shard_map/ppermute | solution.py:306
  15.5 21.1 %collective-permute-start.7 = (f32[128,2048]{1,0:T(8,128)}, f32[128,2048]{1,0:T(8,128)}, u32[]{:S(2)}, u32[]{:S(2)}) collective-permute-start(f32[128,2048]{1,0:T(8,128)} %slice.63), channel_id=1, source_target_pairs={{0,16},{4,20},{1,17},{5,21},{2,18},{6,22},{3,19},{7,23}} | collective-permute-start | bytes 3145736 | tf_op jit(solution)/shard_map/ppermute | solution.py:306
  19.4 13.8 %collective-permute-start.3 = (f32[64,2048]{1,0:T(8,128)}, f32[64,2048]{1,0:T(8,128)}, u32[]{:S(2)}, u32[]{:S(2)}) collective-permute-start(f32[64,2048]{1,0:T(8,128)} %slice_select_fusion.1), channel_id=1, source_target_pairs={{0,8},{4,12},{8,0},{12,4},{16,24},{20,28},{24,16},{28,20},{1,9},{5... | collective-permute-start | bytes 1572872 | tf_op jit(solution)/shard_map/ppermute | solution.py:286
  20.1 2.5 %collective-permute-start.10 = (f32[128,128]{1,0:T(8,128)S(1)}, f32[128,128]{1,0:T(8,128)S(1)}, u32[]{:S(2)}, u32[]{:S(2)}) collective-permute-start(f32[128,128]{1,0:T(8,128)S(1)} %slice_select_fusion.3), channel_id=1, source_target_pairs={{0,4},{4,0},{8,12},{12,8},{16,20},{20,16},{24,28},{28,24},{1,5},{5... | collective-permute-start | bytes 196616 | tf_op jit(solution)/shard_map/ppermute | solution.py:286
  21.3 22.3 %collective-permute-start.14 = (f32[128,128]{1,0:T(8,128)S(1)}, f32[128,128]{1,0:T(8,128)S(1)}, u32[]{:S(2)}, u32[]{:S(2)}) collective-permute-start(f32[128,128]{1,0:T(8,128)S(1)} %broadcast_select_fusion.15), channel_id=1, source_target_pairs={{0,8},{4,12},{16,24},{20,28},{1,9},{5,13},{17,25},{21,29},{2,10},{... | collective-permute-start | bytes 196616 | tf_op jit(solution)/shard_map/ppermute | solution.py:306
  22.7 20.6 %collective-permute-start.11 = (f32[128,128]{1,0:T(8,128)S(1)}, f32[128,128]{1,0:T(8,128)S(1)}, u32[]{:S(2)}, u32[]{:S(2)}) collective-permute-start(f32[128,128]{1,0:T(8,128)S(1)} %select_add_fusion.3), channel_id=1, source_target_pairs={{0,8},{4,12},{8,0},{12,4},{16,24},{20,28},{24,16},{28,20},{1,9},{5... | collective-permute-start | bytes 196616 | tf_op jit(solution)/shard_map/ppermute | solution.py:286
  34.3 7.6 %collective-permute-start.4 = (f32[32,2048]{1,0:T(8,128)S(1)}, f32[32,2048]{1,0:T(8,128)S(1)}, u32[]{:S(2)}, u32[]{:S(2)}) collective-permute-start(f32[32,2048]{1,0:T(8,128)S(1)} %slice_select_fusion.2), channel_id=1, source_target_pairs={{0,16},{4,20},{8,24},{12,28},{16,0},{20,4},{24,8},{28,12},{1,17},{... | collective-permute-start | bytes 786440 | tf_op jit(solution)/shard_map/ppermute | solution.py:286
  38.3 30.2 %collective-permute-start.8 = (f32[128,2048]{1,0:T(8,128)S(1)}, f32[128,2048]{1,0:T(8,128)S(1)}, u32[]{:S(2)}, u32[]{:S(2)}) collective-permute-start(f32[128,2048]{1,0:T(8,128)S(1)} %broadcast_select_fusion.2), channel_id=1, source_target_pairs={{0,8},{4,12},{16,24},{20,28},{1,9},{5,13},{17,25},{21,29},{2,10},{... | collective-permute-start | bytes 3145736 | tf_op jit(solution)/shard_map/ppermute | solution.py:306
  42.0 7.4 %collective-permute-start.5 = (f32[32,2048]{1,0:T(8,128)S(1)}, f32[32,2048]{1,0:T(8,128)S(1)}, u32[]{:S(2)}, u32[]{:S(2)}) collective-permute-start(f32[32,2048]{1,0:T(8,128)S(1)} %select_add_fusion.2), channel_id=1, source_target_pairs={{0,16},{4,20},{8,24},{12,28},{16,0},{20,4},{24,8},{28,12},{1,17},{... | collective-permute-start | bytes 786440 | tf_op jit(solution)/shard_map/ppermute | solution.py:286
  43.3 6.1 %collective-permute-start.12 = (f32[128,128]{1,0:T(8,128)S(1)}, f32[128,128]{1,0:T(8,128)S(1)}, u32[]{:S(2)}, u32[]{:S(2)}) collective-permute-start(f32[128,128]{1,0:T(8,128)S(1)} %add.64), channel_id=1, source_target_pairs={{0,16},{4,20},{8,24},{12,28},{16,0},{20,4},{24,8},{28,12},{1,17},{... | collective-permute-start | bytes 196616 | tf_op jit(solution)/shard_map/ppermute | solution.py:286
  49.5 30.2 %collective-permute-start.6 = (f32[64,2048]{1,0:T(8,128)S(1)}, f32[64,2048]{1,0:T(8,128)S(1)}, u32[]{:S(2)}, u32[]{:S(2)}) collective-permute-start(f32[64,2048]{1,0:T(8,128)S(1)} %pad_maximum_fusion.2), channel_id=1, source_target_pairs={{0,8},{4,12},{8,0},{12,4},{16,24},{20,28},{24,16},{28,20},{1,9},{5... | collective-permute-start | bytes 1572872 | tf_op jit(solution)/shard_map/ppermute | solution.py:286
  81.4 81.1 %collective-permute-start.9 = (f32[1,2,128,2048]{3,2,1,0:T(8,128)}, f32[1,2,128,2048]{3,2,1,0:T(8,128)}, u32[]{:S(2)}, u32[]{:S(2)}) collective-permute-start(f32[1,2,128,2048]{3,2,1,0:T(8,128)} %maximum_bitcast_fusion), channel_id=1, source_target_pairs={{0,4},{4,0},{8,12},{12,8},{16,20},{20,16},{24,28},{28,24},{1,5},{5... | collective-permute-start | bytes 6291464 | tf_op jit(solution)/shard_map/ppermute | solution.py:286
  83.4 7.9 %collective-permute-start.15 = (f32[256,128]{1,0:T(8,128)S(1)}, f32[256,128]{1,0:T(8,128)S(1)}, u32[]{:S(2)}, u32[]{:S(2)}) collective-permute-start(f32[256,128]{1,0:T(8,128)S(1)} %pad_maximum_fusion.4), channel_id=1, source_target_pairs={{0,2},{1,3},{4,6},{5,7},{8,10},{9,11},{12,14},{13,15},{16,18},{17,... | collective-permute-start | bytes 393224 | tf_op jit(solution)/shard_map/ppermute | solution.py:306
  86.6 32.7 %collective-permute-start = (f32[1024,128]{1,0:T(8,128)}, f32[1024,128]{1,0:T(8,128)S(1)}, u32[]{:S(2)}, u32[]{:S(2)}) collective-permute-start(f32[1024,128]{1,0:T(8,128)} %slice.56), channel_id=1, source_target_pairs={{0,2},{1,3},{4,6},{5,7},{8,10},{9,11},{12,14},{13,15},{16,18},{17,... | collective-permute-start | bytes 1572872 | tf_op jit(solution)/shard_map/ppermute | solution.py:306
  91.3 27.4 %collective-permute-start.16 = (f32[256,128]{1,0:T(8,128)S(1)}, f32[256,128]{1,0:T(8,128)S(1)}, u32[]{:S(2)}, u32[]{:S(2)}) collective-permute-start(f32[256,128]{1,0:T(8,128)S(1)} %broadcast_select_fusion.12), channel_id=1, source_target_pairs={{0,1},{1,0},{2,3},{3,2},{4,5},{5,4},{6,7},{7,6},{8,9},{9,8},{10,11... | collective-permute-start | bytes 393224 | tf_op jit(solution)/shard_map/ppermute | solution.py:286
  118.7 4.5 %collective-permute-start.17 = (f32[1,256,256]{2,1,0:T(8,128)S(1)}, f32[1,256,256]{2,1,0:T(8,128)S(1)}, u32[]{:S(2)}, u32[]{:S(2)}) collective-permute-start(f32[1,256,256]{2,1,0:T(8,128)S(1)} %maximum_bitcast_fusion.2), channel_id=1, source_target_pairs={{0,4},{4,0},{8,12},{12,8},{16,20},{20,16},{24,28},{28,24},{1,5},{5... | collective-permute-start | bytes 786440 | tf_op jit(solution)/shard_map/ppermute | solution.py:286
  120.4 41.0 %collective-permute-start.1 = (f32[1024,128]{1,0:T(8,128)S(1)}, f32[1024,128]{1,0:T(8,128)S(1)}, u32[]{:S(2)}, u32[]{:S(2)}) collective-permute-start(f32[1024,128]{1,0:T(8,128)S(1)} %broadcast_select_fusion.5), channel_id=1, source_target_pairs={{0,1},{1,0},{2,3},{3,2},{4,5},{5,4},{6,7},{7,6},{8,9},{9,8},{10,11... | collective-permute-start | bytes 1572872 | tf_op jit(solution)/shard_map/ppermute | solution.py:286
